TPU v7x, 32 devices: a whole 2x2x4 slice. The times are simulated.
32 devices in a mesh: groups: 2 (over y), wide: 4 (over z), narrow: 4 (over x, core).
Axes of the slice: x: 2, y: 2, z: 4, core: 2. Of those that a mesh axis runs over, the one named last changes fastest.
Arguments:
- target_states: bfloat16 [256, 8192], P(('groups', 'wide'), 'narrow'), parts along dimension 0, may hold values from -6 to 6
- source_states: bfloat16 [256, 8192], P(('groups', 'wide'), 'narrow'), parts along dimension 0, may hold values from -6 to 6
- target_gate: bfloat16 [8192, 14336], P('narrow', 'wide'), may hold values from -0.0625 to 0.0625
- target_up: bfloat16 [8192, 14336], P('narrow', 'wide'), may hold values from -0.0625 to 0.0625
- source_gate: bfloat16 [8192, 14336], P('narrow', 'wide'), may hold values from -0.0625 to 0.0625
- source_up: bfloat16 [8192, 14336], P('narrow', 'wide'), may hold values from -0.0625 to 0.0625
- token_ids: int32 [256], P(('groups', 'narrow')), parts along dimension 0, may hold values from 0 to 128255
- lengths: int32 [16], P(('groups', 'narrow')), parts along dimension 0, may hold values from 1 to 16
- ratio_weight: float32 [128256], replicated, may hold values from 0.25 to 1
Outputs:
- target_hidden: bfloat16 [256, 14336], P(('groups', 'narrow'), 'wide'), parts along dimension 0
- ratio_hidden: bfloat16 [256, 14336], P(('groups', 'narrow'), 'wide'), parts along dimension 0
There are 2 independent parts, one for each index of `groups`. A program takes and returns all parts, laid end to end along the dimension named above; an argument that names none is the same for every part. Nothing has to cross between parts.
All inputs are finite; a program needn't handle non-finite values.
Results may differ from a plain program's by a relative error of at most 0.02.
Values may be sent and summed in bfloat16 or wider, within the bound.
A program may use at most 128 MiB of HBM per device.

v0:
```python
import jax
import jax.numpy as jnp
from jax import lax
from jax.sharding import PartitionSpec as P


def matmul(left, right):
    return jnp.dot(left, right, preferred_element_type=jnp.float32)


def pair_project(w_gate, w_upper, piece):
    return jnp.concatenate([matmul(piece, w_gate), matmul(piece, w_upper)], axis=1)


def gated(summed, hidden_cols):
    return jax.nn.silu(summed[:, :hidden_cols]) * summed[:, hidden_cols:]


def local(
    target_states,
    source_states,
    target_gate,
    target_up,
    source_gate,
    source_up,
    token_ids,
    lengths,
    ratio_weight,
):
    hidden_cols = target_gate.shape[1]
    own_rows = token_ids.shape[0]
    target_terms = pair_project(
        target_gate, target_up, lax.all_gather(target_states, "wide", axis=0, tiled=True)
    )
    source_terms = pair_project(
        source_gate, source_up, lax.all_gather(source_states, "wide", axis=0, tiled=True)
    )
    target_sum, source_sum = (
        lax.psum_scatter(
            target_terms.astype(jnp.bfloat16), "narrow", scatter_dimension=0, tiled=True
        ).astype(jnp.float32),
        lax.psum_scatter(
            source_terms.astype(jnp.bfloat16), "narrow", scatter_dimension=0, tiled=True
        ).astype(jnp.float32),
    )
    target_act = gated(target_sum, hidden_cols)
    source_act = gated(source_sum, hidden_cols)
    slot_count = own_rows // lengths.shape[0]
    slots = jnp.arange(slot_count, dtype=jnp.int32)
    live = (slots[None, :] < lengths[:, None]).reshape(-1).astype(jnp.float32)
    weight = ratio_weight[token_ids]
    target_out = (live[:, None] * target_act).astype(jnp.bfloat16)
    ratio_out = (live[:, None] * (target_act - weight[:, None] * source_act)).astype(jnp.bfloat16)
    return (target_out, ratio_out)


def solution(mesh):
    placed = (
        P(("groups", "wide"), "narrow"),
        P(("groups", "wide"), "narrow"),
        P("narrow", "wide"),
        P("narrow", "wide"),
        P("narrow", "wide"),
        P("narrow", "wide"),
        P(("groups", "narrow")),
        P(("groups", "narrow")),
        P(),
    )
    return jax.shard_map(
        local,
        mesh=mesh,
        in_specs=placed,
        out_specs=(P(("groups", "narrow"), "wide"), P(("groups", "narrow"), "wide")),
        check_vma=False,
    )
```

profile of v0, /device:TPU:0, one launch (start us, length us, event | category | flops | bytes accessed | tf_op | source)
XLA Modules:
  0.0 110.6 jit_solution(676333890963916121)
XLA Ops:
  7.2 0.0 copy-start
  7.2 0.0 reduce-scatter.3.cloned.1.call-start
  7.2 17.7 %all_gather.6 = bf16[128,2048]{1,0:T(8,128)(2,1)S(1)} all-gather(bf16[32,2048]{1,0:T(8,128)(2,1)} %param.9), channel_id=1, replica_groups=mesh['groups'=2,'wide'=4,'narrow'=4] {'wide'}, dimensions={0}, use_global_device_ids=true | all-gather | bytes 655360 | tf_op jit(solution)/shard_map/all_gather | solution.py:33
  24.9 0.0 copy-start.1
  24.9 7.4 %convolution_convert_fusion.2 = bf16[128,3584]{1,0:T(8,128)(2,1)S(1)} fusion(bf16[128,2048]{1,0:T(8,128)(2,1)S(1)} %all_gather.6, bf16[2048,3584]{1,0:T(8,128)(2,1)} %param.12), kind=kOutput, calls=%fused_computation.3 | convolution fusion | flops 1879506944 | bytes 16121856 | tf_op jit(solution)/shard_map/dot_general | solution.py:8
  32.4 1.9 %copy-done.1 = bf16[2048,3584]{1,0:T(8,128)(2,1)S(1)} copy-done((bf16[2048,3584]{1,0:T(8,128)(2,1)S(1)}, bf16[2048,3584]{1,0:T(8,128)(2,1)}, u32[]{:S(2)}) %copy-start.1) | copy-done | bytes 14680088
  34.3 2.2 %convolution_convert_fusion.3 = bf16[128,3584]{1,0:T(8,128)(2,1)S(1)} fusion(bf16[128,2048]{1,0:T(8,128)(2,1)S(1)} %all_gather.6, bf16[2048,3584]{1,0:T(8,128)(2,1)S(1)} %copy-done.1), kind=kOutput, calls=%fused_computation.4 | convolution fusion | flops 1879506944 | bytes 16121856 | tf_op jit(solution)/shard_map/dot_general | solution.py:8
  36.5 0.0 copy-start.2
  36.5 1.4 %pad_maximum_fusion = bf16[128,7168]{1,0:T(8,128)(2,1)} fusion(bf16[128,3584]{1,0:T(8,128)(2,1)S(1)} %convolution_convert_fusion.2, bf16[128,3584]{1,0:T(8,128)(2,1)S(1)} %convolution_convert_fusion.3), kind=kLoop, calls=%fused_computation.5 | loop fusion | flops 3670016 | bytes 3670016 | tf_op jit(solution)/shard_map/concatenate | solution.py:12
  37.9 0.0 reduce-scatter.3.cloned.1.call-update
  37.9 0.0 reduce-scatter.5.cloned.1.call-start
  38.0 0.0 copy-done.2
  38.0 16.3 %all_gather.7 = bf16[128,2048]{1,0:T(8,128)(2,1)S(1)} all-gather(bf16[32,2048]{1,0:T(8,128)(2,1)S(1)} %copy-done.2), channel_id=1, replica_groups=mesh['groups'=2,'wide'=4,'narrow'=4] {'wide'}, dimensions={0}, use_global_device_ids=true | all-gather | bytes 655360 | tf_op jit(solution)/shard_map/all_gather | solution.py:36
  54.2 7.6 %convolution_convert_fusion = bf16[128,3584]{1,0:T(8,128)(2,1)S(1)} fusion(bf16[128,2048]{1,0:T(8,128)(2,1)S(1)} %all_gather.7, bf16[2048,3584]{1,0:T(8,128)(2,1)} %param.14), kind=kOutput, calls=%fused_computation.1 | convolution fusion | flops 1879506944 | bytes 16121856 | tf_op jit(solution)/shard_map/dot_general | solution.py:8
  61.8 7.3 %convolution_convert_fusion.1 = bf16[128,3584]{1,0:T(8,128)(2,1)S(1)} fusion(bf16[128,2048]{1,0:T(8,128)(2,1)S(1)} %all_gather.7, bf16[2048,3584]{1,0:T(8,128)(2,1)} %param.13), kind=kOutput, calls=%fused_computation.2 | convolution fusion | flops 1879506944 | bytes 16121856 | tf_op jit(solution)/shard_map/dot_general | solution.py:8
  69.1 0.0 copy-start.3
  69.2 0.0 copy-start.4
  69.2 1.4 %pad_maximum_fusion.1 = bf16[128,7168]{1,0:T(8,128)(2,1)} fusion(bf16[128,3584]{1,0:T(8,128)(2,1)S(1)} %convolution_convert_fusion, bf16[128,3584]{1,0:T(8,128)(2,1)S(1)} %convolution_convert_fusion.1), kind=kLoop, calls=%fused_computation.6 | loop fusion | flops 3670016 | bytes 3670016 | tf_op jit(solution)/shard_map/concatenate | solution.py:12
  70.6 0.0 reduce-scatter.5.cloned.1.call-update
  70.6 0.0 copy-done.3
  70.6 0.1 compare_convert_fusion
  70.7 0.1 reshape.22
  70.8 0.0 copy-done.4
  70.8 0.0 copy-done
  70.8 0.7 gather_fusion
  71.5 0.0 reduce-scatter.3.cloned.1.call-done
  71.5 1.1 convert_element_type.26
  72.6 29.0 %reduce-scatter.5.cloned.1.call-done = bf16[32,7168]{1,0:T(8,128)(2,1)} async-done(((bf16[128,7168]{1,0:T(8,128)(2,1)}), bf16[32,7168]{1,0:T(8,128)(2,1)}) %reduce-scatter.5.cloned.1.call-update) | async-done | bytes 458768 | tf_op jit(solution)/shard_map/reduce_scatter | solution.py:42
  101.6 1.1 convert_element_type.28
  102.7 1.1 fusion.3
  (2 shorter events, 0.0 us)
Async XLA Ops:
  7.2 63.6 %copy-start = (f32[128256]{0:T(1024)S(1)}, f32[128256]{0:T(1024)}, u32[]{:S(2)}) copy-start(f32[128256]{0:T(1024)} %param.17) | copy-start | bytes 1539076
  7.2 64.3 %reduce-scatter.3.cloned.1.call-start = ((), (), s32[]{:S(2)}) async-start(), calls=%async_computation.2 | async-start | bytes 2293760 | tf_op jit(solution)/shard_map/reduce_scatter | solution.py:39
  24.9 9.3 %copy-start.1 = (bf16[2048,3584]{1,0:T(8,128)(2,1)S(1)}, bf16[2048,3584]{1,0:T(8,128)(2,1)}, u32[]{:S(2)}) copy-start(bf16[2048,3584]{1,0:T(8,128)(2,1)} %param.11) | copy-start | bytes 44040196
  36.5 1.5 %copy-start.2 = (bf16[32,2048]{1,0:T(8,128)(2,1)S(1)}, bf16[32,2048]{1,0:T(8,128)(2,1)}, u32[]{:S(2)}) copy-start(bf16[32,2048]{1,0:T(8,128)(2,1)} %param.10) | copy-start | bytes 393220
  37.9 63.7 %reduce-scatter.5.cloned.1.call-start = ((), (), s32[]{:S(2)}) async-start(), calls=%async_computation.3 | async-start | bytes 2293760 | tf_op jit(solution)/shard_map/reduce_scatter | solution.py:42
  69.1 1.5 %copy-start.3 = (s32[2]{0:T(128)S(1)}, s32[2]{0:T(128)}, u32[]{:S(2)}) copy-start(s32[2]{0:T(128)} %param.16) | copy-start | bytes 28
  69.2 1.6 %copy-start.4 = (s32[32]{0:T(128)S(1)}, s32[32]{0:T(128)}, u32[]{:S(2)}) copy-start(s32[32]{0:T(128)} %param.15) | copy-start | bytes 388
Sparse Core Ops, SparseCore 0:
  38.0 31.3 reduce-scatter.2
  71.9 29.5 reduce-scatter.4
where the time goes:
time: 111 us
  blocking collectives  34 us (31%)
  waiting for transfers between devices  29 us (26%)
  matrix products  24.5 us (22%)
  between operations  14.1 us (13%)
  other arithmetic  6.17 us (6%)
  local copies, waits for them, and re-layouts  2.74 us (2%)
    reduce_scatter x1, waiting for transfers between devices, local(): lax.psum_scatter(source_terms.astype(jnp.bfloat16), 'narrow', scatter_dim...  29 us
    dot_general x4, matrix products, matmul(): return jnp.dot(left, right, preferred_element_type=jnp.float32)  24.5 us
    all_gather x1, blocking collectives, local(): lax.all_gather(target_states, 'wide', axis=0, tiled=True)  17.7 us
    all_gather x1, blocking collectives, local(): lax.all_gather(source_states, 'wide', axis=0, tiled=True)  16.3 us
    concatenate x2, other arithmetic, pair_project(): jnp.concatenate([matmul(piece, w_gate), matmul(piece, w_upper)], axis=1)  2.84 us
  transfers between devices with their start and end apart: 2, of which 1 were waited for; matrix products, arithmetic and copies ran while one was open for 17% of the time, Pallas kernels for 0%

commit v1 on v0

--- a/solution.py
+++ b/solution.py
@@ -1,7 +1,14 @@
+import functools
+
 import jax
 import jax.numpy as jnp
 from jax import lax
+from jax.experimental import pallas as pl
+from jax.experimental.pallas import tpu as pltpu
 from jax.sharding import PartitionSpec as P
+
+MESH = pl.DeviceIdType.MESH
+VMEM_BYTES = 67_000_000
 
 
 def matmul(left, right):
@@ -16,7 +23,266 @@
     return jax.nn.silu(summed[:, :hidden_cols]) * summed[:, hidden_cols:]
 
 
+def kernel(
+    wide, tn, slots,
+    live_ref, weight_ref, ts_ref, ss_ref, tg_ref, tu_ref, sg_ref, su_ref,
+    t_out, r_out,
+    gath, wbuf, part, a_send, a_recv, b_send, b_recv, kept,
+    own_sem, g_send, g_recv, w_sem, as_sem, ar_sem, bs_sem, br_sem,
+):
+    w = lax.axis_index("wide")
+    n = lax.axis_index("narrow")
+    x = n // 2
+    c = n % 2
+    mate = 2 * x + (1 - c)
+    across = 2 * (1 - x) + c
+    cols = tg_ref.shape[1]
+    per = cols // tn
+    units = 2 * per
+    rows = part.shape[3]
+
+    def weight_copies(u, slot, model, j):
+        pair = (tg_ref, tu_ref) if model == 0 else (sg_ref, su_ref)
+        span = pl.ds(pl.multiple_of(j * tn, tn), tn)
+        return [
+            pltpu.make_async_copy(pair[k].at[:, span], wbuf.at[slot, k], w_sem.at[slot, k])
+            for k in range(2)
+        ]
+
+    def load(u):
+        slot = u % slots
+
+        @pl.when(u < per)
+        def _():
+            for copy in weight_copies(u, slot, 0, u):
+                copy.start()
+
+        @pl.when(jnp.logical_and(u >= per, u < units))
+        def _():
+            for copy in weight_copies(u, slot, 1, u - per):
+                copy.start()
+
+    own = [
+        pltpu.make_async_copy(ref, gath.at[m, w], own_sem.at[m])
+        for m, ref in enumerate((ts_ref, ss_ref))
+    ]
+    for copy in own:
+        copy.start()
+    for u in range(min(slots, units)):
+        for copy in weight_copies(u, u, u // per, u % per):
+            copy.start()
+
+    barrier = pltpu.get_barrier_semaphore()
+
+    def greet(axis, index):
+        pl.semaphore_signal(barrier, inc=1, device_id={axis: index}, device_id_type=MESH)
+
+    greet("narrow", mate)
+    greet("narrow", across)
+
+    @pl.when(w > 0)
+    def _():
+        greet("wide", w - 1)
+
+    @pl.when(w < wide - 1)
+    def _():
+        greet("wide", w + 1)
+
+    inner = jnp.logical_and(w > 0, w < wide - 1)
+    pl.semaphore_wait(barrier, jnp.where(inner, 4, 3))
+
+    def hop(m, block, up):
+        return pltpu.make_async_remote_copy(
+            src_ref=gath.at[m, block],
+            dst_ref=gath.at[m, block],
+            send_sem=g_send.at[m, 0 if up else 1, block],
+            recv_sem=g_recv.at[m, block],
+            device_id={"wide": w + 1 if up else w - 1},
+            device_id_type=MESH,
+        )
+
+    def gather_step(m, s):
+        @pl.when(w - s >= 0)
+        def _():
+            if s > 0:
+                hop(m, w - s, True).wait_recv()
+
+            @pl.when(w < wide - 1)
+            def _():
+                hop(m, w - s, True).start()
+
+        @pl.when(w + s <= wide - 1)
+        def _():
+            if s > 0:
+                hop(m, w + s, False).wait_recv()
+
+            @pl.when(w > 0)
+            def _():
+                hop(m, w + s, False).start()
+
+        if m == 0:
+            @pl.when(jnp.logical_and(w == s, w < wide - 1))
+            def _():
+                hop(1, w, True).start()
+
+            @pl.when(jnp.logical_and(wide - 1 - w == s, w > 0))
+            def _():
+                hop(1, w, False).start()
+
+    for copy in own:
+        copy.wait()
+    for s in range(wide):
+        gather_step(0, s)
+
+    def a_copy(u):
+        return pltpu.make_async_remote_copy(
+            src_ref=a_send.at[u], dst_ref=a_recv.at[u],
+            send_sem=as_sem.at[u], recv_sem=ar_sem.at[u],
+            device_id={"narrow": mate}, device_id_type=MESH,
+        )
+
+    def b_copy(u):
+        return pltpu.make_async_remote_copy(
+            src_ref=b_send.at[u], dst_ref=b_recv.at[u],
+            send_sem=bs_sem.at[u], recv_sem=br_sem.at[u],
+            device_id={"narrow": across}, device_id_type=MESH,
+        )
+
+    def cross(u):
+        a_copy(u).wait_recv()
+        for k in range(2):
+            total = part[u, k, across] + a_recv[u, 1 - x, k].astype(jnp.float32)
+            b_send[u, k] = total.astype(jnp.bfloat16)
+        b_copy(u).start()
+
+    def unit(u, carry):
+        for s in range(1, wide):
+            @pl.when(u == min(1 + 2 * s, per))
+            def _():
+                gather_step(1, s)
+
+        slot = u % slots
+        model = u // per
+        left = gath[model].reshape(4 * rows, gath.shape[3])
+        for k in range(2):
+            weight_copies(u, slot, 0, 0)[k].wait()
+            part[u, k] = matmul(left, wbuf[slot, k]).reshape(4, rows, tn)
+        load(u + slots)
+        for i in range(2):
+            for k in range(2):
+                a_send[u, i, k] = part[u, k, 2 * i + 1 - c].astype(jnp.bfloat16)
+        a_copy(u).start()
+
+        @pl.when(u > 0)
+        def _():
+            cross(u - 1)
+
+        return carry
+
+    lax.fori_loop(0, units, unit, 0)
+    cross(units - 1)
+
+    def summed(u, k):
+        near = part[u, k, n] + a_recv[u, x, k].astype(jnp.float32)
+        return near + b_recv[u, k].astype(jnp.float32)
+
+    def activation(u):
+        b_copy(u).wait_recv()
+        gate = summed(u, 0)
+        return gate / (1.0 + jnp.exp(-gate)) * summed(u, 1)
+
+    def finish_target(j, carry):
+        act = activation(j)
+        kept[j] = act
+        t_out[:, pl.ds(pl.multiple_of(j * tn, tn), tn)] = (live_ref[...] * act).astype(t_out.dtype)
+        return carry
+
+    def finish_ratio(j, carry):
+        act = activation(per + j)
+        ratio = live_ref[...] * (kept[j] - weight_ref[...] * act)
+        r_out[:, pl.ds(pl.multiple_of(j * tn, tn), tn)] = ratio.astype(r_out.dtype)
+        return carry
+
+    lax.fori_loop(0, per, finish_target, 0)
+    lax.fori_loop(0, per, finish_ratio, 0)
+
+    def drain(u, carry):
+        a_copy(u).wait_send()
+        b_copy(u).wait_send()
+        return carry
+
+    lax.fori_loop(0, units, drain, 0)
+    for m in range(2):
+        for block in range(wide):
+            @pl.when(jnp.logical_and(block <= w, w < wide - 1))
+            def _():
+                hop(m, block, True).wait_send()
+
+            @pl.when(jnp.logical_and(block >= w, w > 0))
+            def _():
+                hop(m, block, False).wait_send()
+
+
+def plan(states, weights, wide, narrow):
+    cols = weights.shape[1]
+    tokens = states.shape[0] * wide
+    if narrow != 4 or wide < 2 or tokens % 64 or states.shape[0] % 16:
+        return None
+    for tn in (512, 256):
+        if cols % tn:
+            continue
+        units = 2 * cols // tn
+        unit_bytes = tn * tokens * 2 * (4 + 1 + 1 + 1)
+        fixed = 2 * tokens * states.shape[1] * 2 + cols * tokens * 4 + units * unit_bytes
+        slots = (VMEM_BYTES - 8_000_000 - fixed) // (4 * tn * states.shape[1])
+        slots = min(slots, units)
+        if slots >= 2:
+            return tn, slots
+    return None
+
+
+def fused(states, weights, live, weight, wide, tn, slots):
+    rows = states[0].shape[0] * wide // 4
+    depth = states[0].shape[1]
+    cols = weights[0].shape[1]
+    units = 2 * cols // tn
+    vmem = pl.BlockSpec(memory_space=pltpu.VMEM)
+    hbm = pl.BlockSpec(memory_space=pl.ANY)
+    out = jax.ShapeDtypeStruct((rows, cols), jnp.bfloat16)
+    dma = pltpu.SemaphoreType.DMA
+    return pl.pallas_call(
+        functools.partial(kernel, wide, tn, slots),
+        out_shape=(out, out),
+        in_specs=[vmem, vmem] + [hbm] * 6,
+        out_specs=(vmem, vmem),
+        scratch_shapes=[
+            pltpu.VMEM((2, wide, states[0].shape[0], depth), jnp.bfloat16),
+            pltpu.VMEM((slots, 2, depth, tn), jnp.bfloat16),
+            pltpu.VMEM((units, 2, 4, rows, tn), jnp.float32),
+            pltpu.VMEM((units, 2, 2, rows, tn), jnp.bfloat16),
+            pltpu.VMEM((units, 2, 2, rows, tn), jnp.bfloat16),
+            pltpu.VMEM((units, 2, rows, tn), jnp.bfloat16),
+            pltpu.VMEM((units, 2, rows, tn), jnp.bfloat16),
+            pltpu.VMEM((units // 2, rows, tn), jnp.float32),
+            dma((2,)),
+            dma((2, 2, wide)),
+            dma((2, wide)),
+            dma((slots, 2)),
+            dma((units,)),
+            dma((units,)),
+            dma((units,)),
+            dma((units,)),
+        ],
+        compiler_params=pltpu.CompilerParams(
+            collective_id=0, has_side_effects=True, vmem_limit_bytes=VMEM_BYTES
+        ),
+        name="rescore",
+    )(live, weight, *states, *weights)
+
+
 def local(
+    wide,
+    narrow,
     target_states,
     source_states,
     target_gate,
@@ -29,6 +295,20 @@
 ):
     hidden_cols = target_gate.shape[1]
     own_rows = token_ids.shape[0]
+    slot_count = own_rows // lengths.shape[0]
+    slots = jnp.arange(slot_count, dtype=jnp.int32)
+    live = (slots[None, :] < lengths[:, None]).reshape(-1).astype(jnp.float32)
+    weight = ratio_weight[token_ids]
+    chosen = plan(target_states, target_gate, wide, narrow)
+    if chosen is not None:
+        return fused(
+            (target_states, source_states),
+            (target_gate, target_up, source_gate, source_up),
+            live[:, None],
+            weight[:, None],
+            wide,
+            *chosen,
+        )
     target_terms = pair_project(
         target_gate, target_up, lax.all_gather(target_states, "wide", axis=0, tiled=True)
     )
@@ -45,10 +325,6 @@
     )
     target_act = gated(target_sum, hidden_cols)
     source_act = gated(source_sum, hidden_cols)
-    slot_count = own_rows // lengths.shape[0]
-    slots = jnp.arange(slot_count, dtype=jnp.int32)
-    live = (slots[None, :] < lengths[:, None]).reshape(-1).astype(jnp.float32)
-    weight = ratio_weight[token_ids]
     target_out = (live[:, None] * target_act).astype(jnp.bfloat16)
     ratio_out = (live[:, None] * (target_act - weight[:, None] * source_act)).astype(jnp.bfloat16)
     return (target_out, ratio_out)
@@ -67,7 +343,7 @@
         P(),
     )
     return jax.shard_map(
-        local,
+        functools.partial(local, mesh.shape["wide"], mesh.shape["narrow"]),
         mesh=mesh,
         in_specs=placed,
         out_specs=(P(("groups", "narrow"), "wide"), P(("groups", "narrow"), "wide")),

time: 111 us -> 65.3 us (0.59)
  Pallas kernels: 0 us -> 56.5 us
  blocking collectives: 34 us -> 0 us
  waiting for transfers between devices: 29 us -> 0 us
  matrix products: 24.5 us -> 0 us
  between operations: 14.1 us -> 0.64 us
  other arithmetic: 6.17 us -> 1.39 us
  local copies, waits for them, and re-layouts: 2.74 us -> 6.41 us
    pallas_call x0 -> x1, Pallas kernels: none -> 56.5 us  [fused(): pl.pallas_call(functools.partial(kernel, wide, tn, slots), out_shape=(out...]
    all_gather x2 -> x0, blocking collectives: 34 us -> none  [the longest x1 17.7 us: local(): lax.all_gather(target_states, 'wide', axis=0, tiled=True)]
    reduce_scatter x2 -> x0, waiting for transfers between devices: 29 us -> none  [the longest x1 29 us: local(): lax.psum_scatter(source_terms.astype(jnp.bfloat16), 'narrow', scatter_dim...]
    dot_general x4 -> x0, matrix products: 24.5 us -> none  [matmul(): return jnp.dot(left, right, preferred_element_type=jnp.float32)]
    convert_element_type x3 -> x0, other arithmetic: 3.24 us -> none  [the longest x2 2.16 us: local(): target_sum, source_sum = (lax.psum_scatter(target_terms.astype(jnp.bfloat...]
    concatenate x2 -> x0, other arithmetic: 2.84 us -> none  [pair_project(): jnp.concatenate([matmul(piece, w_gate), matmul(piece, w_upper)], axis=1)]
    unnamed x10 -> x2, local copies, waits for them, and re-layouts: 1.96 us -> 3.28 us
  transfers between devices with their start and end apart: 2 -> 0, of which waited for: 1 -> 0; matrix products, arithmetic and copies ran while one was open for 17% -> 0% of each run, Pallas kernels for 0% -> 0%
where the time goes in v1:
time: 65.3 us; the launch traced here: 65 us
  Pallas kernels  56.5 us (87%)
  local copies, waits for them, and re-layouts  6.41 us (10%)
  other arithmetic  1.39 us (2%)
    pallas_call x1, Pallas kernels, fused(): pl.pallas_call(functools.partial(kernel, wide, tn, slots), out_shape=(out...  56.5 us
    unnamed x2, local copies, waits for them, and re-layouts  3.28 us
    gather x1, local copies, waits for them, and re-layouts, local(): weight = ratio_weight[token_ids]  1.74 us

profile of v1, /device:TPU:0, one launch (start us, length us, event | category | flops | bytes accessed | tf_op | source)
XLA Modules:
  0.0 65.0 jit_solution(3682242400906690455)
XLA Ops:
  0.6 0.7 %compare_select_fusion = s32[32]{0:T(128)S(1)} fusion(s32[32]{0:T(128)} %param.15), kind=kLoop, calls=%fused_computation.2 | loop fusion | flops 96 | bytes 256 | tf_op jit(solution)/shard_map/select_n | solution.py:301
  1.3 0.7 %compare_convert_fusion = f32[2,16]{1,0:T(2,128)S(1)} fusion(s32[2]{0:T(128)} %param.16), kind=kLoop, calls=%fused_computation.3 | loop fusion | flops 64 | bytes 136 | tf_op jit(solution)/shard_map/convert_element_type | solution.py:300
  2.0 1.7 %gather_fusion = f32[32]{0:T(128)S(1)} fusion(f32[128256]{0:T(1024)} %param.17, s32[1024]{0:T(1024)S(1)} %pad_clamp_fusion), kind=kCustom, calls=%fused_computation | custom fusion | bytes 384 | tf_op jit(solution)/shard_map/gather | solution.py:301
  3.8 0.7 %reshape.41.live_ref = f32[32,1]{1,0:T(8,128)} reshape(f32[2,16]{1,0:T(2,128)S(1)} %compare_convert_fusion) | data formatting | bytes 256 | tf_op jit(solution)/shard_map/convert_element_type | solution.py:300
  4.5 0.7 %copy.14.weight_ref = f32[32,1]{1,0:T(8,128)} copy(f32[32,1]{0,1:T(1,128)S(1)} %bitcast.1) | data formatting | bytes 256 | tf_op jit(solution)/shard_map/broadcast_in_dim | solution.py:308
  5.1 56.5 %rescore.1 = (bf16[32,3584]{1,0:T(8,128)(2,1)}, bf16[32,3584]{1,0:T(8,128)(2,1)}) custom-call(f32[32,1]{1,0:T(8,128)} %reshape.41.live_ref, f32[32,1]{1,0:T(8,128)} %copy.14.weight_ref, bf16[32,2048]{1,0:T(8,128)(2,1)} %ts_ref.1, bf16[32,2048]{1,0:T(8,128)(2,1)} %ss_ref.1, bf16[2048,3584]{1,0:T(8,128)(2,1)} %tg_ref.1, bf16[2048,3584]{1,0:T(8,128)(2,1)} %tu_ref.1, ...), custom_call_target="tpu_custom_call" | custom-call | tf_op jit(solution)/shard_map/rescore/pallas_call | solution.py:253
  61.7 1.6 %copy.17 = bf16[32,3584]{1,0:T(8,128)(2,1)} copy(bf16[32,3584]{1,0:T(8,128)(2,1)} %get-tuple-element.4) | data formatting | bytes 458752
  63.3 1.6 %copy.18 = bf16[32,3584]{1,0:T(8,128)(2,1)} copy(bf16[32,3584]{1,0:T(8,128)(2,1)} %get-tuple-element.5) | data formatting | bytes 458752
  (1 shorter events, 0.0 us)

commit v2 on v1

--- a/solution.py
+++ b/solution.py
@@ -25,10 +25,10 @@
 
 def kernel(
     wide, tn, slots,
-    live_ref, weight_ref, ts_ref, ss_ref, tg_ref, tu_ref, sg_ref, su_ref,
+    ids_ref, len_ref, table_ref, ts_ref, ss_ref, tg_ref, tu_ref, sg_ref, su_ref,
     t_out, r_out,
     gath, wbuf, part, a_send, a_recv, b_send, b_recv, kept,
-    own_sem, g_send, g_recv, w_sem, as_sem, ar_sem, bs_sem, br_sem,
+    live_ref, weight_ref, table, table_sem, own_sem, g_send, g_recv, w_sem, as_sem, ar_sem, bs_sem, br_sem,
 ):
     w = lax.axis_index("wide")
     n = lax.axis_index("narrow")
@@ -41,7 +41,7 @@
     units = 2 * per
     rows = part.shape[3]
 
-    def weight_copies(u, slot, model, j):
+    def weight_copies(slot, model, j):
         pair = (tg_ref, tu_ref) if model == 0 else (sg_ref, su_ref)
         span = pl.ds(pl.multiple_of(j * tn, tn), tn)
         return [
@@ -54,12 +54,12 @@
 
         @pl.when(u < per)
         def _():
-            for copy in weight_copies(u, slot, 0, u):
+            for copy in weight_copies(slot, 0, u):
                 copy.start()
 
         @pl.when(jnp.logical_and(u >= per, u < units))
         def _():
-            for copy in weight_copies(u, slot, 1, u - per):
+            for copy in weight_copies(slot, 1, u - per):
                 copy.start()
 
     own = [
@@ -68,10 +68,15 @@
     ]
     for copy in own:
         copy.start()
-    for u in range(min(slots, units)):
-        for copy in weight_copies(u, u, u // per, u % per):
-            copy.start()
-
+
+    def load_ahead(first, last):
+        for u in range(first, min(last, slots, units)):
+            for copy in weight_copies(u, u // per, u % per):
+                copy.start()
+
+    load_ahead(0, 1)
+    fetch = pltpu.make_async_copy(table_ref, table, table_sem)
+    fetch.start()
     barrier = pltpu.get_barrier_semaphore()
 
     def greet(axis, index):
@@ -131,8 +136,10 @@
 
     for copy in own:
         copy.wait()
+    batch = pl.cdiv(slots - 1, wide)
     for s in range(wide):
         gather_step(0, s)
+        load_ahead(1 + s * batch, 1 + (s + 1) * batch)
 
     def a_copy(u):
         return pltpu.make_async_remote_copy(
@@ -165,9 +172,8 @@
         model = u // per
         left = gath[model].reshape(4 * rows, gath.shape[3])
         for k in range(2):
-            weight_copies(u, slot, 0, 0)[k].wait()
+            weight_copies(slot, 0, 0)[k].wait()
             part[u, k] = matmul(left, wbuf[slot, k]).reshape(4, rows, tn)
-        load(u + slots)
         for i in range(2):
             for k in range(2):
                 a_send[u, i, k] = part[u, k, 2 * i + 1 - c].astype(jnp.bfloat16)
@@ -177,10 +183,24 @@
         def _():
             cross(u - 1)
 
+        load(u + slots)
         return carry
 
     lax.fori_loop(0, units, unit, 0)
     cross(units - 1)
+
+    fetch.wait()
+    row = lax.broadcasted_iota(jnp.int32, (rows, 1), 0)
+    hlen = rows // len_ref.shape[0]
+    lived = jnp.zeros((rows, 1), jnp.float32)
+    for h in range(len_ref.shape[0]):
+        inside = jnp.logical_and(row >= h * hlen, row < h * hlen + len_ref[h])
+        lived = jnp.where(inside, 1.0, lived)
+    weights = jnp.zeros((rows, 1), jnp.float32)
+    for i in range(rows):
+        weights = jnp.where(row == i, table[ids_ref[i]], weights)
+    live_ref[...] = lived
+    weight_ref[...] = weights
 
     def summed(u, k):
         near = part[u, k, n] + a_recv[u, x, k].astype(jnp.float32)
@@ -221,6 +241,19 @@
             @pl.when(jnp.logical_and(block >= w, w > 0))
             def _():
                 hop(m, block, False).wait_send()
+
+
+def hand_over(*refs):
+    taken, given, held, in_sem, out_sem = refs[:2], refs[2:4], refs[4], refs[5], refs[6]
+    arrive = [pltpu.make_async_copy(taken[i], held.at[i], in_sem.at[i]) for i in range(2)]
+    leave = [pltpu.make_async_copy(held.at[i], given[i], out_sem.at[i]) for i in range(2)]
+    for copy in arrive:
+        copy.start()
+    for i in range(2):
+        arrive[i].wait()
+        leave[i].start()
+    for copy in leave:
+        copy.wait()
 
 
 def plan(states, weights, wide, narrow):
@@ -241,19 +274,20 @@
     return None
 
 
-def fused(states, weights, live, weight, wide, tn, slots):
+def fused(states, weights, token_ids, lengths, ratio_weight, wide, tn, slots):
     rows = states[0].shape[0] * wide // 4
     depth = states[0].shape[1]
     cols = weights[0].shape[1]
     units = 2 * cols // tn
+    smem = pl.BlockSpec(memory_space=pltpu.SMEM)
     vmem = pl.BlockSpec(memory_space=pltpu.VMEM)
     hbm = pl.BlockSpec(memory_space=pl.ANY)
     out = jax.ShapeDtypeStruct((rows, cols), jnp.bfloat16)
     dma = pltpu.SemaphoreType.DMA
-    return pl.pallas_call(
+    pair = pl.pallas_call(
         functools.partial(kernel, wide, tn, slots),
         out_shape=(out, out),
-        in_specs=[vmem, vmem] + [hbm] * 6,
+        in_specs=[smem, smem] + [hbm] * 7,
         out_specs=(vmem, vmem),
         scratch_shapes=[
             pltpu.VMEM((2, wide, states[0].shape[0], depth), jnp.bfloat16),
@@ -264,6 +298,10 @@
             pltpu.VMEM((units, 2, rows, tn), jnp.bfloat16),
             pltpu.VMEM((units, 2, rows, tn), jnp.bfloat16),
             pltpu.VMEM((units // 2, rows, tn), jnp.float32),
+            pltpu.VMEM((rows, 1), jnp.float32),
+            pltpu.VMEM((rows, 1), jnp.float32),
+            pltpu.SMEM(ratio_weight.shape, jnp.float32),
+            dma,
             dma((2,)),
             dma((2, 2, wide)),
             dma((2, wide)),
@@ -277,7 +315,15 @@
             collective_id=0, has_side_effects=True, vmem_limit_bytes=VMEM_BYTES
         ),
         name="rescore",
-    )(live, weight, *states, *weights)
+    )(token_ids, lengths, ratio_weight, *states, *weights)
+    return pl.pallas_call(
+        hand_over,
+        out_shape=(out, out),
+        in_specs=[hbm, hbm],
+        out_specs=(hbm, hbm),
+        scratch_shapes=[pltpu.VMEM((2, rows, cols), jnp.bfloat16), dma((2,)), dma((2,))],
+        name="hand_over",
+    )(*pair)
 
 
 def local(
@@ -295,20 +341,21 @@
 ):
     hidden_cols = target_gate.shape[1]
     own_rows = token_ids.shape[0]
-    slot_count = own_rows // lengths.shape[0]
-    slots = jnp.arange(slot_count, dtype=jnp.int32)
-    live = (slots[None, :] < lengths[:, None]).reshape(-1).astype(jnp.float32)
-    weight = ratio_weight[token_ids]
     chosen = plan(target_states, target_gate, wide, narrow)
     if chosen is not None:
         return fused(
             (target_states, source_states),
             (target_gate, target_up, source_gate, source_up),
-            live[:, None],
-            weight[:, None],
+            token_ids,
+            lengths,
+            ratio_weight,
             wide,
             *chosen,
         )
+    slot_count = own_rows // lengths.shape[0]
+    slots = jnp.arange(slot_count, dtype=jnp.int32)
+    live = (slots[None, :] < lengths[:, None]).reshape(-1).astype(jnp.float32)
+    weight = ratio_weight[token_ids]
     target_terms = pair_project(
         target_gate, target_up, lax.all_gather(target_states, "wide", axis=0, tiled=True)
     )

time: 65.3 us -> 48 us (0.74)
  Pallas kernels: 56.5 us -> 47.2 us
  local copies, waits for them, and re-layouts: 6.41 us -> 0 us
  other arithmetic: 1.39 us -> 0 us
    pallas_call x1, Pallas kernels: 56.5 us -> 45.4 us  [fused(): pl.pallas_call(functools.partial(kernel, wide, tn, slots), out_shape=(out...]
    unnamed x2 -> x0, local copies, waits for them, and re-layouts: 3.28 us -> none
    pallas_call x0 -> x1, Pallas kernels: none -> 1.77 us  [fused(): pl.pallas_call(hand_over, out_shape=(out, out), in_specs=[hbm, hbm], out_...]
    gather x1 -> x0, local copies, waits for them, and re-layouts: 1.74 us -> none  [local(): weight = ratio_weight[token_ids]]
    convert_element_type x1 -> x0, other arithmetic: 0.72 us -> none  [local(): live = (slots[None, :] < lengths[:, None]).reshape(-1).astype(jnp.float32)]
    convert_element_type x1 -> x0, local copies, waits for them, and re-layouts: 0.7 us -> none  [local(): live = (slots[None, :] < lengths[:, None]).reshape(-1).astype(jnp.float32)]
    broadcast_in_dim x1 -> x0, local copies, waits for them, and re-layouts: 0.69 us -> none  [local(): weight[:, None]]
    select_n x1 -> x0, other arithmetic: 0.66 us -> none  [local(): weight = ratio_weight[token_ids]]
where the time goes in v2:
time: 48 us; the launch traced here: 47.8 us
  Pallas kernels  47.2 us (98%)
  between operations  0.64 us (1%)
    pallas_call x1, Pallas kernels, fused(): pl.pallas_call(functools.partial(kernel, wide, tn, slots), out_shape=(out...  45.4 us
    pallas_call x1, Pallas kernels, fused(): pl.pallas_call(hand_over, out_shape=(out, out), in_specs=[hbm, hbm], out_...  1.77 us

profile of v2, /device:TPU:0, one launch (start us, length us, event | category | flops | bytes accessed | tf_op | source)
XLA Modules:
  0.0 47.8 jit_solution(3300493943839764547)
XLA Ops:
  0.6 45.4 %rescore.1 = (bf16[32,3584]{1,0:T(8,128)(2,1)}, bf16[32,3584]{1,0:T(8,128)(2,1)}) custom-call(s32[32]{0:T(128)} %ids_ref.1, s32[2]{0:T(128)} %len_ref.1, f32[128256]{0:T(1024)} %table_ref.1, bf16[32,2048]{1,0:T(8,128)(2,1)} %ts_ref.1, bf16[32,2048]{1,0:T(8,128)(2,1)} %ss_ref.1, bf16[2048,3584]{1,0:T(8,128)(2,1)} %tg_ref.1, bf16[2048,3584]{1,0:T(8,128)(2,1)} %tu_ref.1, ...), custom_call_target="tpu_custom_call" | custom-call | tf_op jit(solution)/shard_map/rescore/pallas_call | solution.py:287
  46.1 1.8 %hand_over.1 = (bf16[32,3584]{1,0:T(8,128)(2,1)}, bf16[32,3584]{1,0:T(8,128)(2,1)}) custom-call(bf16[32,3584]{1,0:T(8,128)(2,1)} %get-tuple-element.4.refs_0_, bf16[32,3584]{1,0:T(8,128)(2,1)} %get-tuple-element.5.refs_1_), custom_call_target="tpu_custom_call" | custom-call | tf_op jit(solution)/shard_map/hand_over/pallas_call | solution.py:319

commit v3 on v2

--- a/solution.py
+++ b/solution.py
@@ -76,7 +76,6 @@
 
     load_ahead(0, 1)
     fetch = pltpu.make_async_copy(table_ref, table, table_sem)
-    fetch.start()
     barrier = pltpu.get_barrier_semaphore()
 
     def greet(axis, index):
@@ -140,6 +139,7 @@
     for s in range(wide):
         gather_step(0, s)
         load_ahead(1 + s * batch, 1 + (s + 1) * batch)
+    fetch.start()
 
     def a_copy(u):
         return pltpu.make_async_remote_copy(
@@ -268,7 +268,7 @@
         unit_bytes = tn * tokens * 2 * (4 + 1 + 1 + 1)
         fixed = 2 * tokens * states.shape[1] * 2 + cols * tokens * 4 + units * unit_bytes
         slots = (VMEM_BYTES - 8_000_000 - fixed) // (4 * tn * states.shape[1])
-        slots = min(slots, units)
+        slots = min(slots, units, 1 + 2 * wide)
         if slots >= 2:
             return tn, slots
     return None

time: 48 us -> 48 us (level)
  no operation moved by 1% of the time
where the time goes in v3:
time: 48 us; the launch traced here: 47.8 us
  Pallas kernels  47.2 us (98%)
  between operations  0.64 us (1%)
    pallas_call x1, Pallas kernels, fused(): pl.pallas_call(functools.partial(kernel, wide, tn, slots), out_shape=(out...  45.4 us
    pallas_call x1, Pallas kernels, fused(): pl.pallas_call(hand_over, out_shape=(out, out), in_specs=[hbm, hbm], out_...  1.77 us

profile of v3, /device:TPU:0, one launch (start us, length us, event | category | flops | bytes accessed | tf_op | source)
XLA Modules:
  0.0 47.8 jit_solution(9746649719019284732)
XLA Ops:
  0.6 45.4 %rescore.1 = (bf16[32,3584]{1,0:T(8,128)(2,1)}, bf16[32,3584]{1,0:T(8,128)(2,1)}) custom-call(s32[32]{0:T(128)} %ids_ref.1, s32[2]{0:T(128)} %len_ref.1, f32[128256]{0:T(1024)} %table_ref.1, bf16[32,2048]{1,0:T(8,128)(2,1)} %ts_ref.1, bf16[32,2048]{1,0:T(8,128)(2,1)} %ss_ref.1, bf16[2048,3584]{1,0:T(8,128)(2,1)} %tg_ref.1, bf16[2048,3584]{1,0:T(8,128)(2,1)} %tu_ref.1, ...), custom_call_target="tpu_custom_call" | custom-call | tf_op jit(solution)/shard_map/rescore/pallas_call | solution.py:287
  46.1 1.8 %hand_over.1 = (bf16[32,3584]{1,0:T(8,128)(2,1)}, bf16[32,3584]{1,0:T(8,128)(2,1)}) custom-call(bf16[32,3584]{1,0:T(8,128)(2,1)} %get-tuple-element.4.refs_0_, bf16[32,3584]{1,0:T(8,128)(2,1)} %get-tuple-element.5.refs_1_), custom_call_target="tpu_custom_call" | custom-call | tf_op jit(solution)/shard_map/hand_over/pallas_call | solution.py:319
